TPU v7x, 32 devices: a whole 2x2x4 slice. The times are simulated.
32 devices in a mesh: tm: 4 (over y, x), space: 8 (over z, core).
Axes of the slice: x: 2, y: 2, z: 4, core: 2. Of those that a mesh axis runs over, the one named last changes fastest.
Arguments:
- signal: bfloat16 [16, 256, 512], P('space', None, 'tm'), may hold values from -6 to 6
- source_boxes: int32 [16, 12], replicated, may hold values from 0 to 15
- near_boxes: int32 [16, 8], replicated, may hold values from 0 to 15, as said below
- trans_kernel: float32 [12, 256, 128], P(None, 'space'), may hold values from -0.15625 to 0.15625
- near_kernel: float32 [8, 128], replicated, may hold values from -0.1875 to 0.1875
Outputs:
- field: bfloat16 [16, 256, 512], P('space', None, 'tm')
Inputs may be any that keep to these rules, and one draw needn't show every extreme that they name: Each near_boxes[b, j] lies within 2 of b.
All inputs are finite; a program needn't handle non-finite values.
Results may differ from a plain program's by a relative error of at most 0.008.
Values may be sent and summed in bfloat16 or wider, within the bound.
A program may use at most 192 MiB of HBM per device.

v0:
```python
import functools

import jax
import jax.numpy as jnp
from jax import lax
from jax.experimental import pallas as pl
from jax.experimental.pallas import tpu as pltpu
from jax.sharding import PartitionSpec as P

REACH = 2
MESH = pl.DeviceIdType.MESH
LANES = 128
SUBLANES = 8
def from_behind(shard, axis, by):
    size = lax.axis_size(axis)
    pairs = [(i, i + by) for i in range(size) if 0 <= i + by < size]
    return lax.ppermute(shard, axis, pairs)


def with_halo(block, sides, width):
    for axis, dim in sides:
        count = lax.axis_size(axis)
        forward = [(i, i + 1) for i in range(count - 1)]
        backward = [(target, source) for source, target in forward]
        low = lax.ppermute(
            lax.slice_in_dim(block, block.shape[dim] - width, None, axis=dim), axis, forward
        )
        high = lax.ppermute(lax.slice_in_dim(block, 0, width, axis=dim), axis, backward)
        block = jnp.concatenate([low, block, high], axis=dim)
    return block


def block_matrix(kernel):
    blocklen = kernel.shape[-1]
    leading = kernel.shape[:-1]
    zeroes = jnp.zeros(leading + (2 * blocklen,), jnp.bfloat16)
    widened = jnp.concatenate([zeroes, kernel.astype(jnp.bfloat16)], axis=-1)
    tiled = jnp.tile(widened, (1,) * len(leading) + (2 * blocklen,))
    trimmed = tiled[..., : 2 * blocklen * (3 * blocklen - 1)]
    skewed = trimmed.reshape(leading + (2 * blocklen, 3 * blocklen - 1))
    return skewed[..., :blocklen]


def body(signal, source_boxes, near_boxes, trans_kernel, near_kernel):
    box_dev = signal.shape[0]
    current_rays = lax.all_to_all(signal, "space", split_axis=1, concat_axis=0, tiled=True)
    earlier_rays = from_behind(current_rays, "tm", 1)
    pair_rays = jnp.concatenate([earlier_rays, current_rays], axis=-1)
    offsets = source_boxes.shape[1]
    far = jnp.zeros(current_rays.shape, jnp.float32)
    for offset in range(offsets):
        trans_mats = block_matrix(trans_kernel[offset])
        rows = jnp.take(pair_rays, source_boxes[:, offset], axis=0)
        far = far + jnp.einsum("brs,rst->brt", rows, trans_mats, preferred_element_type=jnp.float32)
    far_rays = far.astype(jnp.bfloat16)
    near_mats = block_matrix(near_kernel)
    slots = near_boxes.shape[1]
    earlier_box = from_behind(signal, "tm", 1)
    pair_box = jnp.concatenate([earlier_box, signal], axis=-1)
    padded = with_halo(pair_box, (("space", 0),), REACH)
    first = lax.axis_index("space") * box_dev
    own_near = lax.dynamic_slice_in_dim(near_boxes, first, box_dev, 0)
    local_rows = own_near - (first - REACH)
    near_sum = jnp.zeros(signal.shape, jnp.float32)
    for slot in range(slots):
        rows = jnp.take(padded, local_rows[:, slot], axis=0)
        near_sum = near_sum + jnp.einsum(
            "brs,st->brt", rows, near_mats[slot], preferred_element_type=jnp.float32
        )
    near_box = near_sum.astype(jnp.bfloat16)
    far_box = lax.all_to_all(far_rays, "space", split_axis=0, concat_axis=1, tiled=True)
    return (far_box.astype(jnp.float32) + near_box.astype(jnp.float32)).astype(jnp.bfloat16)


def fused_kernel(
    n_tm,
    n_space,
    signal_ref,
    source_ref,
    near_ref,
    trans_ref,
    kernel_ref,
    out_ref,
    staged,
    landed,
    wide,
    flat,
    trans_rows,
    near_rows,
    trans_mats,
    near_mats,
    far_all,
    near_all,
    leaving,
    sources,
    nears,
    in_send,
    in_recv,
    out_send,
    out_recv,
    local_sem,
    stage_sem,
):
    tm, space = lax.axis_index("tm"), lax.axis_index("space")
    peers = n_tm * n_space
    box_dev = signal_ref.shape[0]
    boxes = n_space * box_dev
    offsets = trans_ref.shape[0]
    slots = kernel_ref.shape[0]
    rows = n_tm * boxes
    block_rows = boxes * SUBLANES

    def wrapped(value, size):
        return jnp.where(value >= size, value - size, value)

    order = sorted(range(n_space), key=lambda ds: -min(ds, n_space - ds))
    others = [
        (wrapped(tm + dt, n_tm), wrapped(space + ds, n_space))
        for ds in order
        for dt in reversed(range(n_tm))
        if dt or ds
    ]
    mine = space * n_tm + tm
    own_boxes = pl.ds(space * box_dev, box_dev)

    first_ray = pl.multiple_of(tm * SUBLANES, SUBLANES)
    fetches = [
        pltpu.make_async_copy(
            trans_ref.at[:, pl.ds(first_ray, SUBLANES), :], trans_rows, local_sem.at[0]
        ),
        pltpu.make_async_copy(kernel_ref, near_rows, local_sem.at[1]),
        pltpu.make_async_copy(source_ref, sources, local_sem.at[2]),
        pltpu.make_async_copy(near_ref, nears, local_sem.at[3]),
    ]
    stagings = [
        pltpu.make_async_copy(signal_ref.at[nth], staged.at[:, nth], stage_sem.at[nth])
        for nth in range(box_dev)
    ]
    for fetch in stagings:
        fetch.start()
    barrier = pltpu.get_barrier_semaphore()
    for other in others:
        pl.semaphore_signal(barrier, inc=1, device_id=other, device_id_type=MESH)
    for fetch in fetches:
        fetch.start()
    pltpu.make_async_copy(signal_ref.at[:, mine], landed.at[tm + 1, own_boxes], in_recv).start()
    for staging in stagings:
        staging.wait()
    pl.semaphore_wait(barrier, peers - 1)
    for other in others:
        pltpu.make_async_remote_copy(
            src_ref=staged.at[other[1] * n_tm + other[0]],
            dst_ref=landed.at[tm + 1, own_boxes],
            send_sem=in_send,
            recv_sem=in_recv,
            device_id=other,
            device_id_type=MESH,
        ).start()

    lag = lax.broadcasted_iota(jnp.int32, (LANES, LANES), 1) - lax.broadcasted_iota(
        jnp.int32, (LANES, LANES), 0
    )
    causal = lag >= 0

    def split_rows(response):
        spread = jnp.broadcast_to(response, (LANES, LANES))
        turned = pltpu.roll(spread, 0, 1, stride=1, stride_axis=0)
        now = jnp.where(causal, turned, 0.0).astype(jnp.bfloat16)
        before = jnp.where(causal, 0.0, turned).astype(jnp.bfloat16)
        return before, now

    for fetch in fetches:
        fetch.wait()

    def build(offset, carry):
        responses = trans_rows[offset]
        column = pl.ds(pl.multiple_of(offset * LANES, LANES), LANES)
        for ray in range(SUBLANES):
            before, now = split_rows(responses[ray : ray + 1, :])
            trans_mats[ray, 0:LANES, column] = before
            trans_mats[ray, LANES : 2 * LANES, column] = now
        return carry

    lax.fori_loop(0, offsets, build, 0)
    for slot in range(slots):
        before, now = split_rows(near_rows[slot : slot + 1, :])
        near_mats[0:LANES, slot * LANES : (slot + 1) * LANES] = before
        near_mats[LANES : 2 * LANES, slot * LANES : (slot + 1) * LANES] = now
    wide[0:block_rows, :] = jnp.zeros((block_rows, LANES), jnp.float32)
    flat[0:block_rows, :] = jnp.zeros((block_rows, LANES), jnp.bfloat16)

    arrived = landed.at[pl.ds(1, n_tm)]
    pltpu.make_async_copy(arrived, arrived, in_recv).wait()

    for block in range(1, n_tm + 1):
        these = landed[block].astype(jnp.float32).reshape(block_rows, LANES)
        wide[block * block_rows : (block + 1) * block_rows, :] = these
        flat[block * block_rows : (block + 1) * block_rows, :] = these.astype(jnp.bfloat16)

    far_rows = far_all.reshape(offsets, rows * SUBLANES, LANES)
    for ray in range(SUBLANES):
        blocks = wide[pl.ds(ray, rows + boxes, stride=SUBLANES), :].astype(jnp.bfloat16)
        pair = jnp.concatenate([blocks[:rows], blocks[boxes:]], axis=1)
        products = jnp.dot(pair, trans_mats[ray], preferred_element_type=jnp.float32)
        for offset in range(offsets):
            far_rows[offset, pl.ds(ray, rows, stride=SUBLANES), :] = products[
                :, offset * LANES : (offset + 1) * LANES
            ]

    for tile in range(0, slots, 2):
        taken = min(2, slots - tile)
        products = jnp.dot(
            jnp.concatenate(
                [flat[0 : n_tm * block_rows, :], flat[block_rows:, :]], axis=1
            ),
            near_mats[:, tile * LANES : (tile + taken) * LANES],
            preferred_element_type=jnp.float32,
        )
        for nth in range(taken):
            near_all[tile + nth] = products[:, nth * LANES : (nth + 1) * LANES].reshape(
                rows, SUBLANES, LANES
            )

    def selected(all_ref, table, count, box, block, by_slot):
        total = None
        for entry in range(count):
            origin = table[entry, box] if by_slot else table[box, entry]
            term = all_ref[entry, origin + block * boxes]
            total = term if total is None else total + term
        return total.astype(jnp.bfloat16).astype(jnp.float32)

    def finish(to_space):
        for nth in range(box_dev):
            box = to_space * box_dev + nth
            for block in range(n_tm):
                far = selected(far_all, sources, offsets, box, block, False)
                near = selected(near_all, nears, slots, box, block, True)
                leaving[block, box] = (far + near).astype(jnp.bfloat16)

    def dispatch(ds):
        to_space = wrapped(space + ds, n_space)
        to_boxes = pl.ds(to_space * box_dev, box_dev)
        for dt in range(n_tm):
            to_tm = wrapped(tm + dt, n_tm)
            if dt or ds:
                pltpu.make_async_remote_copy(
                    src_ref=leaving.at[to_tm, to_boxes],
                    dst_ref=out_ref.at[:, mine],
                    send_sem=out_send,
                    recv_sem=out_recv,
                    device_id=(to_tm, to_space),
                    device_id_type=MESH,
                ).start()
            else:
                pltpu.make_async_copy(
                    leaving.at[tm, to_boxes], out_ref.at[:, mine], out_recv
                ).start()

    for nth, ds in enumerate(order):
        finish(wrapped(space + ds, n_space))
        if nth:
            dispatch(order[nth - 1])
    dispatch(order[-1])

    sent = staged.at[pl.ds(0, peers - 1)]
    pltpu.make_async_copy(sent, sent, in_send).wait()
    pltpu.make_async_copy(out_ref, out_ref, out_recv).wait()
    pltpu.make_async_copy(sent, sent, out_send).wait()


def fused_body(signal, source_boxes, near_boxes, trans_kernel, near_kernel):
    n_tm, n_space = lax.axis_size("tm"), lax.axis_size("space")
    peers = n_tm * n_space
    box_dev, rays, samples = signal.shape
    boxes = box_dev * n_space
    offsets, slots = trans_kernel.shape[0], near_kernel.shape[0]
    rows = n_tm * boxes
    grouped = signal.reshape(box_dev, peers, SUBLANES, samples)
    hbm = pl.BlockSpec(memory_space=pltpu.HBM)
    field = pl.pallas_call(
        functools.partial(fused_kernel, n_tm, n_space),
        out_shape=pltpu.VMEM(grouped.shape, jnp.bfloat16),
        in_specs=[hbm] * 5,
        out_specs=pl.BlockSpec(memory_space=pl.ANY),
        scratch_shapes=[
            pltpu.VMEM((peers, box_dev, SUBLANES, LANES), jnp.bfloat16),
            pltpu.VMEM((n_tm + 1, boxes, SUBLANES, LANES), jnp.bfloat16),
            pltpu.VMEM(((rows + boxes) * SUBLANES, LANES), jnp.float32),
            pltpu.VMEM(((rows + boxes) * SUBLANES, LANES), jnp.bfloat16),
            pltpu.VMEM((offsets, SUBLANES, LANES), jnp.float32),
            pltpu.VMEM((slots, LANES), jnp.float32),
            pltpu.VMEM((SUBLANES, 2 * LANES, offsets * LANES), jnp.bfloat16),
            pltpu.VMEM((2 * LANES, slots * LANES), jnp.bfloat16),
            pltpu.VMEM((offsets, rows, SUBLANES, LANES), jnp.float32),
            pltpu.VMEM((slots, rows, SUBLANES, LANES), jnp.float32),
            pltpu.VMEM((n_tm, boxes, SUBLANES, LANES), jnp.bfloat16),
            pltpu.SMEM(source_boxes.shape, jnp.int32),
            pltpu.SMEM(near_boxes.shape[::-1], jnp.int32),
            pltpu.SemaphoreType.DMA,
            pltpu.SemaphoreType.DMA,
            pltpu.SemaphoreType.DMA,
            pltpu.SemaphoreType.DMA,
            pltpu.SemaphoreType.DMA((4,)),
            pltpu.SemaphoreType.DMA((box_dev,)),
        ],
        compiler_params=pltpu.CompilerParams(
            collective_id=0, has_side_effects=True, vmem_limit_bytes=60*1024*1024
        ),
    )(*[pltpu.with_memory_space_constraint(x, pltpu.HBM) for x in (grouped, source_boxes, near_boxes.T, trans_kernel, near_kernel)])
    return field.reshape(signal.shape)


def routed(signal, source_boxes, near_boxes, trans_kernel, near_kernel):
    n_tm, n_space = lax.axis_size("tm"), lax.axis_size("space")
    box_dev, rays, samples = signal.shape
    rows = n_tm * n_space * box_dev
    fits = rays == n_tm * n_space * SUBLANES and samples == LANES and rows <= 2 * LANES
    chosen = fused_body if fits else body
    return chosen(signal, source_boxes, near_boxes, trans_kernel, near_kernel)


def solution(mesh):
    in_specs = (P("space", None, "tm"), P(), P(), P(None, "space", None), P())
    out_specs = P("space", None, "tm")
    return jax.shard_map(
        routed, mesh=mesh, in_specs=in_specs, out_specs=out_specs, check_vma=False
    )
```

profile of v0, /device:TPU:0, one launch (start us, length us, event | category | flops | bytes accessed | tf_op | source)
XLA Modules:
  0.0 20.8 jit_solution(18404476479243632474)
XLA Ops:
  0.0 20.1 %shard_map.55 = bf16[2,32,8,128]{3,2,1,0:T(8,128)(2,1)S(1)} custom-call(bf16[2,32,8,128]{3,2,1,0:T(8,128)(2,1)} %bitcast.4, s32[16,12]{1,0:T(8,128)} %source_ref.1, s32[8,16]{1,0:T(8,128)} %bitcast.5, f32[12,32,128]{2,1,0:T(8,128)} %trans_ref.1, f32[8,128]{1,0:T(8,128)} %kernel_ref.1), custom_call_target="tpu_custom_call" | custom-call | tf_op jit(solution)/shard_map/pallas_call | solution.py:280
  20.1 0.7 %copy.7 = bf16[2,256,128]{2,1,0:T(8,128)(2,1)} copy(bf16[2,256,128]{2,1,0:T(8,128)(2,1)S(1)} %bitcast.3) | data formatting | bytes 262144
where the time goes:
time: 21 us; the launch traced here: 20.8 us
  Pallas kernels  20.1 us (96%)
  local copies, waits for them, and re-layouts  0.66 us (3%)
    pallas_call x1, Pallas kernels, fused_body(): pl.pallas_call(functools.partial(fused_kernel, n_tm, n_space), out_shape=...  20.1 us
    unnamed x1, local copies, waits for them, and re-layouts  0.66 us

commit v1 on v0

v1 whole, which is shorter than its diff:
```python
import functools

import jax
import jax.numpy as jnp
import numpy as np
from jax import lax
from jax.experimental import pallas as pl
from jax.experimental.pallas import tpu as pltpu
from jax.sharding import PartitionSpec as P

REACH = 2
MESH = pl.DeviceIdType.MESH
LANES = 128
SUBLANES = 8
def from_behind(shard, axis, by):
    size = lax.axis_size(axis)
    pairs = [(i, i + by) for i in range(size) if 0 <= i + by < size]
    return lax.ppermute(shard, axis, pairs)


def with_halo(block, sides, width):
    for axis, dim in sides:
        count = lax.axis_size(axis)
        forward = [(i, i + 1) for i in range(count - 1)]
        backward = [(target, source) for source, target in forward]
        low = lax.ppermute(
            lax.slice_in_dim(block, block.shape[dim] - width, None, axis=dim), axis, forward
        )
        high = lax.ppermute(lax.slice_in_dim(block, 0, width, axis=dim), axis, backward)
        block = jnp.concatenate([low, block, high], axis=dim)
    return block


def block_matrix(kernel):
    blocklen = kernel.shape[-1]
    leading = kernel.shape[:-1]
    zeroes = jnp.zeros(leading + (2 * blocklen,), jnp.bfloat16)
    widened = jnp.concatenate([zeroes, kernel.astype(jnp.bfloat16)], axis=-1)
    tiled = jnp.tile(widened, (1,) * len(leading) + (2 * blocklen,))
    trimmed = tiled[..., : 2 * blocklen * (3 * blocklen - 1)]
    skewed = trimmed.reshape(leading + (2 * blocklen, 3 * blocklen - 1))
    return skewed[..., :blocklen]


def body(signal, source_boxes, near_boxes, trans_kernel, near_kernel):
    box_dev = signal.shape[0]
    current_rays = lax.all_to_all(signal, "space", split_axis=1, concat_axis=0, tiled=True)
    earlier_rays = from_behind(current_rays, "tm", 1)
    pair_rays = jnp.concatenate([earlier_rays, current_rays], axis=-1)
    offsets = source_boxes.shape[1]
    far = jnp.zeros(current_rays.shape, jnp.float32)
    for offset in range(offsets):
        trans_mats = block_matrix(trans_kernel[offset])
        rows = jnp.take(pair_rays, source_boxes[:, offset], axis=0)
        far = far + jnp.einsum("brs,rst->brt", rows, trans_mats, preferred_element_type=jnp.float32)
    far_rays = far.astype(jnp.bfloat16)
    near_mats = block_matrix(near_kernel)
    slots = near_boxes.shape[1]
    earlier_box = from_behind(signal, "tm", 1)
    pair_box = jnp.concatenate([earlier_box, signal], axis=-1)
    padded = with_halo(pair_box, (("space", 0),), REACH)
    first = lax.axis_index("space") * box_dev
    own_near = lax.dynamic_slice_in_dim(near_boxes, first, box_dev, 0)
    local_rows = own_near - (first - REACH)
    near_sum = jnp.zeros(signal.shape, jnp.float32)
    for slot in range(slots):
        rows = jnp.take(padded, local_rows[:, slot], axis=0)
        near_sum = near_sum + jnp.einsum(
            "brs,st->brt", rows, near_mats[slot], preferred_element_type=jnp.float32
        )
    near_box = near_sum.astype(jnp.bfloat16)
    far_box = lax.all_to_all(far_rays, "space", split_axis=0, concat_axis=1, tiled=True)
    return (far_box.astype(jnp.float32) + near_box.astype(jnp.float32)).astype(jnp.bfloat16)


def spectral_tables(blocklen):
    lags = np.arange(2 * blocklen)[:, None]
    odd = 2 * np.arange(blocklen)[None, :] + 1
    angle = np.pi * lags * odd / (2 * blocklen)
    forward = np.concatenate([np.cos(angle), -np.sin(angle)], axis=1)
    later = angle[blocklen:].T
    inverse = np.concatenate([np.cos(later), -np.sin(later)], axis=0) / blocklen
    return jnp.asarray(forward, jnp.bfloat16), jnp.asarray(inverse, jnp.bfloat16)


def fused_kernel(
    n_tm,
    n_space,
    signal_ref,
    source_ref,
    near_ref,
    trans_ref,
    kernel_ref,
    forward_ref,
    inverse_ref,
    out_ref,
    staged,
    landed,
    spectra,
    responses,
    trans_rows,
    near_rows,
    forward,
    inverse,
    leaving,
    sources,
    nears,
    in_send,
    in_recv,
    out_send,
    out_recv,
    local_sem,
    stage_sem,
):
    tm, space = lax.axis_index("tm"), lax.axis_index("space")
    peers = n_tm * n_space
    box_dev = signal_ref.shape[0]
    boxes = n_space * box_dev
    offsets = trans_ref.shape[0]
    slots = kernel_ref.shape[0]
    rows = n_tm * boxes

    def skipping(position, mine):
        return position + jnp.where(position >= mine, 1, 0)

    mine = space * n_tm + tm
    own_boxes = pl.ds(space * box_dev, box_dev)
    others = []
    for position in range(peers - 1):
        peer = skipping(position, mine)
        others.append((peer % n_tm, peer // n_tm))

    first_ray = pl.multiple_of(tm * SUBLANES, SUBLANES)
    fetches = [
        pltpu.make_async_copy(
            trans_ref.at[:, pl.ds(first_ray, SUBLANES), :], trans_rows, local_sem.at[0]
        ),
        pltpu.make_async_copy(kernel_ref, near_rows, local_sem.at[1]),
        pltpu.make_async_copy(source_ref, sources, local_sem.at[2]),
        pltpu.make_async_copy(near_ref, nears, local_sem.at[3]),
        pltpu.make_async_copy(forward_ref, forward, local_sem.at[4]),
        pltpu.make_async_copy(inverse_ref, inverse, local_sem.at[5]),
    ]
    stagings = [
        pltpu.make_async_copy(signal_ref.at[nth], staged.at[:, nth], stage_sem.at[nth])
        for nth in range(box_dev)
    ]
    for fetch in stagings:
        fetch.start()
    barrier = pltpu.get_barrier_semaphore()
    for other in others:
        pl.semaphore_signal(barrier, inc=1, device_id=other, device_id_type=MESH)
    for fetch in fetches:
        fetch.start()
    pltpu.make_async_copy(signal_ref.at[:, mine], landed.at[tm + 1, own_boxes], in_recv).start()
    for staging in stagings:
        staging.wait()
    pl.semaphore_wait(barrier, peers - 1)
    for other in reversed(others):
        pltpu.make_async_remote_copy(
            src_ref=staged.at[other[1] * n_tm + other[0]],
            dst_ref=landed.at[tm + 1, own_boxes],
            send_sem=in_send,
            recv_sem=in_recv,
            device_id=other,
            device_id_type=MESH,
        ).start()

    for fetch in fetches:
        fetch.wait()

    def respond(lags):
        return jnp.dot(
            lags.astype(jnp.bfloat16), forward[0:LANES, :], preferred_element_type=jnp.float32
        )

    far_real = respond(trans_rows[...].reshape(offsets * SUBLANES, LANES))
    near_real = respond(near_rows[...])
    for entry in range(offsets + slots):
        if entry < offsets:
            both = far_real[entry * SUBLANES : (entry + 1) * SUBLANES, :]
        else:
            slot = entry - offsets
            both = jnp.broadcast_to(near_real[slot : slot + 1, :], (SUBLANES, 2 * LANES))
        real, imag = both[:, :LANES], both[:, LANES:]
        responses[entry, 0] = real
        responses[entry, 1] = imag - real
        responses[entry, 2] = imag + real
    landed[0] = jnp.zeros(landed.shape[1:], jnp.bfloat16)

    arrived = landed.at[pl.ds(1, n_tm)]
    pltpu.make_async_copy(arrived, arrived, in_recv).wait()

    flat = landed[...].astype(jnp.float32).reshape((rows + boxes) * SUBLANES, LANES)
    flat = flat.astype(jnp.bfloat16)
    pair = jnp.concatenate([flat[: rows * SUBLANES], flat[boxes * SUBLANES :]], axis=1)
    both = jnp.dot(pair, forward[...], preferred_element_type=jnp.float32)
    real = both[:, :LANES].reshape(rows, SUBLANES, LANES)
    imag = both[:, LANES:].reshape(rows, SUBLANES, LANES)
    spectra[0] = real
    spectra[1] = imag
    spectra[2] = real + imag

    def finish(to_space):
        wanted = [(nth, block) for nth in range(box_dev) for block in range(n_tm)]
        sums = {}
        for entry in range(offsets + slots):
            factors = [responses[entry, part] for part in range(3)]
            for nth in range(box_dev):
                box = to_space * box_dev + nth
                origin = sources[box, entry] if entry < offsets else nears[entry - offsets, box]
                for block in range(n_tm):
                    row = origin + block * boxes
                    terms = [
                        factors[0] * spectra[2, row],
                        factors[1] * spectra[0, row],
                        factors[2] * spectra[1, row],
                    ]
                    if entry:
                        terms = [x + y for x, y in zip(sums[nth, block], terms)]
                    sums[nth, block] = terms
        real = jnp.concatenate([sums[w][0] - sums[w][2] for w in wanted], axis=0)
        imag = jnp.concatenate([sums[w][0] + sums[w][1] for w in wanted], axis=0)
        spectrum = jnp.concatenate([real, imag], axis=1).astype(jnp.bfloat16)
        field = jnp.dot(spectrum, inverse[...], preferred_element_type=jnp.float32)
        for place, (nth, block) in enumerate(wanted):
            leaving[block, to_space * box_dev + nth] = field[
                place * SUBLANES : (place + 1) * SUBLANES
            ].astype(jnp.bfloat16)

    def dispatch(to_space, own):
        to_boxes = pl.ds(to_space * box_dev, box_dev)
        for position in range(n_tm - 1 if own else n_tm):
            to_tm = skipping(position, tm) if own else position
            pltpu.make_async_remote_copy(
                src_ref=leaving.at[to_tm, to_boxes],
                dst_ref=out_ref.at[:, mine],
                send_sem=out_send,
                recv_sem=out_recv,
                device_id=(to_tm, to_space),
                device_id_type=MESH,
            ).start()
        if own:
            pltpu.make_async_copy(leaving.at[tm, to_boxes], out_ref.at[:, mine], out_recv).start()

    for position in range(n_space - 1):
        finish(skipping(position, space))
        dispatch(skipping(position, space), False)
    finish(space)
    dispatch(space, True)

    sent = staged.at[pl.ds(0, peers - 1)]
    pltpu.make_async_copy(sent, sent, in_send).wait()
    pltpu.make_async_copy(out_ref, out_ref, out_recv).wait()
    pltpu.make_async_copy(sent, sent, out_send).wait()


def fused_body(signal, source_boxes, near_boxes, trans_kernel, near_kernel):
    n_tm, n_space = lax.axis_size("tm"), lax.axis_size("space")
    peers = n_tm * n_space
    box_dev, rays, samples = signal.shape
    boxes = box_dev * n_space
    offsets, slots = trans_kernel.shape[0], near_kernel.shape[0]
    rows = n_tm * boxes
    grouped = signal.reshape(box_dev, peers, SUBLANES, samples)
    forward, inverse = spectral_tables(samples)
    operands = (
        grouped, source_boxes, near_boxes.T, trans_kernel, near_kernel, forward, inverse
    )
    hbm = pl.BlockSpec(memory_space=pltpu.HBM)
    field = pl.pallas_call(
        functools.partial(fused_kernel, n_tm, n_space),
        out_shape=pltpu.VMEM(grouped.shape, jnp.bfloat16),
        in_specs=[hbm] * len(operands),
        out_specs=pl.BlockSpec(memory_space=pl.ANY),
        scratch_shapes=[
            pltpu.VMEM((peers, box_dev, SUBLANES, LANES), jnp.bfloat16),
            pltpu.VMEM((n_tm + 1, boxes, SUBLANES, LANES), jnp.bfloat16),
            pltpu.VMEM((3, rows, SUBLANES, LANES), jnp.float32),
            pltpu.VMEM((offsets + slots, 3, SUBLANES, LANES), jnp.float32),
            pltpu.VMEM((offsets, SUBLANES, LANES), jnp.float32),
            pltpu.VMEM((slots, LANES), jnp.float32),
            pltpu.VMEM(forward.shape, jnp.bfloat16),
            pltpu.VMEM(inverse.shape, jnp.bfloat16),
            pltpu.VMEM((n_tm, boxes, SUBLANES, LANES), jnp.bfloat16),
            pltpu.SMEM(source_boxes.shape, jnp.int32),
            pltpu.SMEM(near_boxes.shape[::-1], jnp.int32),
            pltpu.SemaphoreType.DMA,
            pltpu.SemaphoreType.DMA,
            pltpu.SemaphoreType.DMA,
            pltpu.SemaphoreType.DMA,
            pltpu.SemaphoreType.DMA((6,)),
            pltpu.SemaphoreType.DMA((box_dev,)),
        ],
        compiler_params=pltpu.CompilerParams(
            collective_id=0, has_side_effects=True, vmem_limit_bytes=60*1024*1024
        ),
    )(*[pltpu.with_memory_space_constraint(x, pltpu.HBM) for x in operands])
    return field.reshape(signal.shape)


def routed(signal, source_boxes, near_boxes, trans_kernel, near_kernel):
    n_tm, n_space = lax.axis_size("tm"), lax.axis_size("space")
    box_dev, rays, samples = signal.shape
    rows = n_tm * n_space * box_dev
    fits = rays == n_tm * n_space * SUBLANES and samples == LANES and rows <= 2 * LANES
    chosen = fused_body if fits else body
    return chosen(signal, source_boxes, near_boxes, trans_kernel, near_kernel)


def solution(mesh):
    in_specs = (P("space", None, "tm"), P(), P(), P(None, "space", None), P())
    out_specs = P("space", None, "tm")
    return jax.shard_map(
        routed, mesh=mesh, in_specs=in_specs, out_specs=out_specs, check_vma=False
    )
```

time: 21 us -> 19.8 us (0.943)
  Pallas kernels: 20.1 us -> 19 us
    pallas_call x1, Pallas kernels: 20.1 us -> 19 us  [fused_body(): pl.pallas_call(functools.partial(fused_kernel, n_tm, n_space), out_shape=...]
where the time goes in v1:
time: 19.8 us; the launch traced here: 19.6 us
  Pallas kernels  19 us (96%)
  local copies, waits for them, and re-layouts  0.66 us (3%)
    pallas_call x1, Pallas kernels, fused_body(): pl.pallas_call(functools.partial(fused_kernel, n_tm, n_space), out_shape=...  19 us
    unnamed x1, local copies, waits for them, and re-layouts  0.66 us

profile of v1, /device:TPU:0, one launch (start us, length us, event | category | flops | bytes accessed | tf_op | source)
XLA Modules:
  0.0 19.6 jit_solution(11030760613745143690)
XLA Ops:
  0.0 19.0 %shard_map.73 = bf16[2,32,8,128]{3,2,1,0:T(8,128)(2,1)S(1)} custom-call(bf16[2,32,8,128]{3,2,1,0:T(8,128)(2,1)} %bitcast.4, s32[16,12]{1,0:T(8,128)} %source_ref.1, s32[8,16]{1,0:T(8,128)} %bitcast.5, f32[12,32,128]{2,1,0:T(8,128)} %trans_ref.1, f32[8,128]{1,0:T(8,128)} %kernel_ref.1, bf16[256,256]{1,0:T(8,128)(2,1)} %constant.4.clone.forward_ref, ...), custom_call_target="tpu_custom_call" | custom-call | tf_op jit(solution)/shard_map/pallas_call | solution.py:271
  19.0 0.7 %copy.9 = bf16[2,256,128]{2,1,0:T(8,128)(2,1)} copy(bf16[2,256,128]{2,1,0:T(8,128)(2,1)S(1)} %bitcast.3) | data formatting | bytes 262144

commit v2 on v1

--- a/solution.py
+++ b/solution.py
@@ -125,10 +125,6 @@
 
     mine = space * n_tm + tm
     own_boxes = pl.ds(space * box_dev, box_dev)
-    others = []
-    for position in range(peers - 1):
-        peer = skipping(position, mine)
-        others.append((peer % n_tm, peer // n_tm))
 
     first_ray = pl.multiple_of(tm * SUBLANES, SUBLANES)
     fetches = [
@@ -145,24 +141,28 @@
         pltpu.make_async_copy(signal_ref.at[nth], staged.at[:, nth], stage_sem.at[nth])
         for nth in range(box_dev)
     ]
+    barrier = pltpu.get_barrier_semaphore()
+    for peer in range(peers):
+        to = (peer % n_tm, peer // n_tm)
+        pl.semaphore_signal(barrier, inc=1, device_id=to, device_id_type=MESH)
     for fetch in stagings:
         fetch.start()
-    barrier = pltpu.get_barrier_semaphore()
-    for other in others:
-        pl.semaphore_signal(barrier, inc=1, device_id=other, device_id_type=MESH)
     for fetch in fetches:
         fetch.start()
-    pltpu.make_async_copy(signal_ref.at[:, mine], landed.at[tm + 1, own_boxes], in_recv).start()
+    pltpu.make_async_copy(
+        signal_ref.at[:, mine], landed.at[tm + 1, own_boxes], in_recv.at[tm]
+    ).start()
     for staging in stagings:
         staging.wait()
-    pl.semaphore_wait(barrier, peers - 1)
-    for other in reversed(others):
+    pl.semaphore_wait(barrier, peers)
+    for position in reversed(range(peers - 1)):
+        peer = skipping(position, mine)
         pltpu.make_async_remote_copy(
-            src_ref=staged.at[other[1] * n_tm + other[0]],
+            src_ref=staged.at[peer],
             dst_ref=landed.at[tm + 1, own_boxes],
             send_sem=in_send,
-            recv_sem=in_recv,
-            device_id=other,
+            recv_sem=in_recv.at[tm],
+            device_id=(peer % n_tm, peer // n_tm),
             device_id_type=MESH,
         ).start()
 
@@ -182,45 +182,41 @@
         else:
             slot = entry - offsets
             both = jnp.broadcast_to(near_real[slot : slot + 1, :], (SUBLANES, 2 * LANES))
-        real, imag = both[:, :LANES], both[:, LANES:]
-        responses[entry, 0] = real
-        responses[entry, 1] = imag - real
-        responses[entry, 2] = imag + real
+        responses[entry, 0] = both[:, :LANES]
+        responses[entry, 1] = both[:, LANES:]
     landed[0] = jnp.zeros(landed.shape[1:], jnp.bfloat16)
 
-    arrived = landed.at[pl.ds(1, n_tm)]
-    pltpu.make_async_copy(arrived, arrived, in_recv).wait()
-
-    flat = landed[...].astype(jnp.float32).reshape((rows + boxes) * SUBLANES, LANES)
-    flat = flat.astype(jnp.bfloat16)
-    pair = jnp.concatenate([flat[: rows * SUBLANES], flat[boxes * SUBLANES :]], axis=1)
-    both = jnp.dot(pair, forward[...], preferred_element_type=jnp.float32)
-    real = both[:, :LANES].reshape(rows, SUBLANES, LANES)
-    imag = both[:, LANES:].reshape(rows, SUBLANES, LANES)
-    spectra[0] = real
-    spectra[1] = imag
-    spectra[2] = real + imag
+    def unpacked(block):
+        flat = landed[block].astype(jnp.float32).reshape(boxes * SUBLANES, LANES)
+        return flat.astype(jnp.bfloat16)
+
+    for block in reversed(range(n_tm)):
+        for arriving in range(block, block - 2, -1):
+            if arriving >= 0 and (arriving < block or block == n_tm - 1):
+                arrived = landed.at[arriving + 1]
+                pltpu.make_async_copy(arrived, arrived, in_recv.at[arriving]).wait()
+        pair = jnp.concatenate([unpacked(block), unpacked(block + 1)], axis=1)
+        both = jnp.dot(pair, forward[...], preferred_element_type=jnp.float32)
+        these = pl.ds(block * boxes, boxes)
+        spectra[0, these] = both[:, :LANES].reshape(boxes, SUBLANES, LANES)
+        spectra[1, these] = both[:, LANES:].reshape(boxes, SUBLANES, LANES)
 
     def finish(to_space):
         wanted = [(nth, block) for nth in range(box_dev) for block in range(n_tm)]
-        sums = {}
+        reals, imags = {}, {}
         for entry in range(offsets + slots):
-            factors = [responses[entry, part] for part in range(3)]
+            c, d = responses[entry, 0], responses[entry, 1]
             for nth in range(box_dev):
                 box = to_space * box_dev + nth
                 origin = sources[box, entry] if entry < offsets else nears[entry - offsets, box]
                 for block in range(n_tm):
-                    row = origin + block * boxes
-                    terms = [
-                        factors[0] * spectra[2, row],
-                        factors[1] * spectra[0, row],
-                        factors[2] * spectra[1, row],
-                    ]
+                    a, b = (spectra[part, origin + block * boxes] for part in range(2))
+                    real, imag = a * c - b * d, a * d + b * c
                     if entry:
-                        terms = [x + y for x, y in zip(sums[nth, block], terms)]
-                    sums[nth, block] = terms
-        real = jnp.concatenate([sums[w][0] - sums[w][2] for w in wanted], axis=0)
-        imag = jnp.concatenate([sums[w][0] + sums[w][1] for w in wanted], axis=0)
+                        real, imag = reals[nth, block] + real, imags[nth, block] + imag
+                    reals[nth, block], imags[nth, block] = real, imag
+        real = jnp.concatenate([reals[w] for w in wanted], axis=0)
+        imag = jnp.concatenate([imags[w] for w in wanted], axis=0)
         spectrum = jnp.concatenate([real, imag], axis=1).astype(jnp.bfloat16)
         field = jnp.dot(spectrum, inverse[...], preferred_element_type=jnp.float32)
         for place, (nth, block) in enumerate(wanted):
@@ -228,10 +224,10 @@
                 place * SUBLANES : (place + 1) * SUBLANES
             ].astype(jnp.bfloat16)
 
-    def dispatch(to_space, own):
+    def dispatch(to_space):
         to_boxes = pl.ds(to_space * box_dev, box_dev)
-        for position in range(n_tm - 1 if own else n_tm):
-            to_tm = skipping(position, tm) if own else position
+
+        def remote(to_tm):
             pltpu.make_async_remote_copy(
                 src_ref=leaving.at[to_tm, to_boxes],
                 dst_ref=out_ref.at[:, mine],
@@ -240,14 +236,24 @@
                 device_id=(to_tm, to_space),
                 device_id_type=MESH,
             ).start()
-        if own:
+
+        for position in range(n_tm - 1):
+            remote(skipping(position, tm))
+
+        @pl.when(space != to_space)
+        def _():
+            remote(tm)
+
+        @pl.when(space == to_space)
+        def _():
             pltpu.make_async_copy(leaving.at[tm, to_boxes], out_ref.at[:, mine], out_recv).start()
 
-    for position in range(n_space - 1):
-        finish(skipping(position, space))
-        dispatch(skipping(position, space), False)
-    finish(space)
-    dispatch(space, True)
+    def serve(to_space, carry):
+        finish(to_space)
+        dispatch(to_space)
+        return carry
+
+    lax.fori_loop(0, n_space, serve, 0)
 
     sent = staged.at[pl.ds(0, peers - 1)]
     pltpu.make_async_copy(sent, sent, in_send).wait()
@@ -276,8 +282,8 @@
         scratch_shapes=[
             pltpu.VMEM((peers, box_dev, SUBLANES, LANES), jnp.bfloat16),
             pltpu.VMEM((n_tm + 1, boxes, SUBLANES, LANES), jnp.bfloat16),
-            pltpu.VMEM((3, rows, SUBLANES, LANES), jnp.float32),
-            pltpu.VMEM((offsets + slots, 3, SUBLANES, LANES), jnp.float32),
+            pltpu.VMEM((2, rows, SUBLANES, LANES), jnp.float32),
+            pltpu.VMEM((offsets + slots, 2, SUBLANES, LANES), jnp.float32),
             pltpu.VMEM((offsets, SUBLANES, LANES), jnp.float32),
             pltpu.VMEM((slots, LANES), jnp.float32),
             pltpu.VMEM(forward.shape, jnp.bfloat16),
@@ -286,7 +292,7 @@
             pltpu.SMEM(source_boxes.shape, jnp.int32),
             pltpu.SMEM(near_boxes.shape[::-1], jnp.int32),
             pltpu.SemaphoreType.DMA,
-            pltpu.SemaphoreType.DMA,
+            pltpu.SemaphoreType.DMA((n_tm,)),
             pltpu.SemaphoreType.DMA,
             pltpu.SemaphoreType.DMA,
             pltpu.SemaphoreType.DMA((6,)),

time: 19.8 us -> 18 us (0.909)
  Pallas kernels: 19 us -> 17.1 us
    pallas_call x1, Pallas kernels: 19 us -> 17.1 us  [fused_body(): pl.pallas_call(functools.partial(fused_kernel, n_tm, n_space), out_shape=...]
where the time goes in v2:
time: 18 us; the launch traced here: 17.7 us
  Pallas kernels  17.1 us (95%)
  local copies, waits for them, and re-layouts  0.66 us (4%)
    pallas_call x1, Pallas kernels, fused_body(): pl.pallas_call(functools.partial(fused_kernel, n_tm, n_space), out_shape=...  17.1 us
    unnamed x1, local copies, waits for them, and re-layouts  0.66 us

profile of v2, /device:TPU:0, one launch (start us, length us, event | category | flops | bytes accessed | tf_op | source)
XLA Modules:
  0.0 17.7 jit_solution(8126078218558711589)
XLA Ops:
  0.0 17.1 %shard_map.73 = bf16[2,32,8,128]{3,2,1,0:T(8,128)(2,1)S(1)} custom-call(bf16[2,32,8,128]{3,2,1,0:T(8,128)(2,1)} %bitcast.4, s32[16,12]{1,0:T(8,128)} %source_ref.1, s32[8,16]{1,0:T(8,128)} %bitcast.5, f32[12,32,128]{2,1,0:T(8,128)} %trans_ref.1, f32[8,128]{1,0:T(8,128)} %kernel_ref.1, bf16[256,256]{1,0:T(8,128)(2,1)} %constant.4.clone.forward_ref, ...), custom_call_target="tpu_custom_call" | custom-call | tf_op jit(solution)/shard_map/pallas_call | solution.py:277
  17.1 0.7 %copy.9 = bf16[2,256,128]{2,1,0:T(8,128)(2,1)} copy(bf16[2,256,128]{2,1,0:T(8,128)(2,1)S(1)} %bitcast.3) | data formatting | bytes 262144

commit v3 on v2

--- a/solution.py
+++ b/solution.py
@@ -182,8 +182,10 @@
         else:
             slot = entry - offsets
             both = jnp.broadcast_to(near_real[slot : slot + 1, :], (SUBLANES, 2 * LANES))
-        responses[entry, 0] = both[:, :LANES]
-        responses[entry, 1] = both[:, LANES:]
+        real, imag = both[:, :LANES], both[:, LANES:]
+        responses[entry, 0] = real
+        responses[entry, 1] = imag - real
+        responses[entry, 2] = imag + real
     landed[0] = jnp.zeros(landed.shape[1:], jnp.bfloat16)
 
     def unpacked(block):
@@ -197,26 +199,25 @@
                 pltpu.make_async_copy(arrived, arrived, in_recv.at[arriving]).wait()
         pair = jnp.concatenate([unpacked(block), unpacked(block + 1)], axis=1)
         both = jnp.dot(pair, forward[...], preferred_element_type=jnp.float32)
-        these = pl.ds(block * boxes, boxes)
-        spectra[0, these] = both[:, :LANES].reshape(boxes, SUBLANES, LANES)
-        spectra[1, these] = both[:, LANES:].reshape(boxes, SUBLANES, LANES)
+        spectra[:, 2 * block] = both[:, :LANES].reshape(boxes, SUBLANES, LANES)
+        spectra[:, 2 * block + 1] = both[:, LANES:].reshape(boxes, SUBLANES, LANES)
 
     def finish(to_space):
         wanted = [(nth, block) for nth in range(box_dev) for block in range(n_tm)]
-        reals, imags = {}, {}
+        sums = {}
         for entry in range(offsets + slots):
-            c, d = responses[entry, 0], responses[entry, 1]
+            factors = [responses[entry, part] for part in range(3)]
             for nth in range(box_dev):
                 box = to_space * box_dev + nth
                 origin = sources[box, entry] if entry < offsets else nears[entry - offsets, box]
                 for block in range(n_tm):
-                    a, b = (spectra[part, origin + block * boxes] for part in range(2))
-                    real, imag = a * c - b * d, a * d + b * c
+                    a, b = (spectra[origin, 2 * block + part] for part in range(2))
+                    terms = [factors[0] * (a + b), factors[1] * a, factors[2] * b]
                     if entry:
-                        real, imag = reals[nth, block] + real, imags[nth, block] + imag
-                    reals[nth, block], imags[nth, block] = real, imag
-        real = jnp.concatenate([reals[w] for w in wanted], axis=0)
-        imag = jnp.concatenate([imags[w] for w in wanted], axis=0)
+                        terms = [x + y for x, y in zip(sums[nth, block], terms)]
+                    sums[nth, block] = terms
+        real = jnp.concatenate([sums[w][0] - sums[w][2] for w in wanted], axis=0)
+        imag = jnp.concatenate([sums[w][0] + sums[w][1] for w in wanted], axis=0)
         spectrum = jnp.concatenate([real, imag], axis=1).astype(jnp.bfloat16)
         field = jnp.dot(spectrum, inverse[...], preferred_element_type=jnp.float32)
         for place, (nth, block) in enumerate(wanted):
@@ -282,8 +283,8 @@
         scratch_shapes=[
             pltpu.VMEM((peers, box_dev, SUBLANES, LANES), jnp.bfloat16),
             pltpu.VMEM((n_tm + 1, boxes, SUBLANES, LANES), jnp.bfloat16),
-            pltpu.VMEM((2, rows, SUBLANES, LANES), jnp.float32),
-            pltpu.VMEM((offsets + slots, 2, SUBLANES, LANES), jnp.float32),
+            pltpu.VMEM((boxes, 2 * n_tm, SUBLANES, LANES), jnp.float32),
+            pltpu.VMEM((offsets + slots, 3, SUBLANES, LANES), jnp.float32),
             pltpu.VMEM((offsets, SUBLANES, LANES), jnp.float32),
             pltpu.VMEM((slots, LANES), jnp.float32),
             pltpu.VMEM(forward.shape, jnp.bfloat16),

time: 18 us -> 17.6 us (0.978)
  Pallas kernels: 17.1 us -> 16.8 us
    pallas_call x1, Pallas kernels: 17.1 us -> 16.8 us  [fused_body(): pl.pallas_call(functools.partial(fused_kernel, n_tm, n_space), out_shape=...]
where the time goes in v3:
time: 17.6 us; the launch traced here: 17.5 us
  Pallas kernels  16.8 us (95%)
  local copies, waits for them, and re-layouts  0.66 us (4%)
    pallas_call x1, Pallas kernels, fused_body(): pl.pallas_call(functools.partial(fused_kernel, n_tm, n_space), out_shape=...  16.8 us
    unnamed x1, local copies, waits for them, and re-layouts  0.66 us

profile of v3, /device:TPU:0, one launch (start us, length us, event | category | flops | bytes accessed | tf_op | source)
XLA Modules:
  0.0 17.5 jit_solution(18433601931655302203)
XLA Ops:
  0.0 16.8 %shard_map.73 = bf16[2,32,8,128]{3,2,1,0:T(8,128)(2,1)S(1)} custom-call(bf16[2,32,8,128]{3,2,1,0:T(8,128)(2,1)} %bitcast.4, s32[16,12]{1,0:T(8,128)} %source_ref.1, s32[8,16]{1,0:T(8,128)} %bitcast.5, f32[12,32,128]{2,1,0:T(8,128)} %trans_ref.1, f32[8,128]{1,0:T(8,128)} %kernel_ref.1, bf16[256,256]{1,0:T(8,128)(2,1)} %constant.4.clone.forward_ref, ...), custom_call_target="tpu_custom_call" | custom-call | tf_op jit(solution)/shard_map/pallas_call | solution.py:278
  16.8 0.7 %copy.9 = bf16[2,256,128]{2,1,0:T(8,128)(2,1)} copy(bf16[2,256,128]{2,1,0:T(8,128)(2,1)S(1)} %bitcast.3) | data formatting | bytes 262144

commit v4 on v3

--- a/solution.py
+++ b/solution.py
@@ -12,6 +12,8 @@
 MESH = pl.DeviceIdType.MESH
 LANES = 128
 SUBLANES = 8
+SHARE = 4
+ORDERS = ((0,3,1,2),(0,1,2,3),(0,1,2,3),(1,0,2,3))
 def from_behind(shard, axis, by):
     size = lax.axis_size(axis)
     pairs = [(i, i + by) for i in range(size) if 0 <= i + by < size]
@@ -98,6 +100,7 @@
     landed,
     spectra,
     responses,
+    near_responses,
     trans_rows,
     near_rows,
     forward,
@@ -111,26 +114,66 @@
     out_recv,
     local_sem,
     stage_sem,
+    ready,
 ):
     tm, space = lax.axis_index("tm"), lax.axis_index("space")
     peers = n_tm * n_space
+    last = n_tm - 1
     box_dev = signal_ref.shape[0]
     boxes = n_space * box_dev
     offsets = trans_ref.shape[0]
     slots = kernel_ref.shape[0]
-    rows = n_tm * boxes
+    on_first, on_last = tm == 0, tm == last
+    on_edge = jnp.logical_or(on_first, on_last)
+    on_middle = jnp.logical_not(on_edge)
+
+    orders = ORDERS
+    def awaited(line, turn):
+        def needs(item):
+            if line in (0, last) and item == last:
+                return {0, last + 2} if line else {last + 1}
+            shift = 1 if line == last else 0
+            return {item + shift, item + 1 + shift} - ({0} if line < last else set())
+
+        before = [needs(item) for item in orders[line][:turn]]
+        return sorted(needs(orders[line][turn]).difference(*before))
+
+    def item_at(turn):
+        item = orders[0][turn]
+        for line in range(1, n_tm):
+            item = jnp.where(tm == line, orders[line][turn], item)
+        return item
+
+    def swapped(item):
+        return jnp.logical_and(on_edge, item == last)
+
+    def group_of(item):
+        return jnp.where(swapped(item), last - tm, tm)
+
+    def places(item):
+        shift = jnp.where(on_last, 1, 0)
+        return jnp.where(swapped(item), 0, item + shift), item + 1 + shift
 
     def skipping(position, mine):
         return position + jnp.where(position >= mine, 1, 0)
 
-    mine = space * n_tm + tm
     own_boxes = pl.ds(space * box_dev, box_dev)
-
-    first_ray = pl.multiple_of(tm * SUBLANES, SUBLANES)
+    barrier = pltpu.get_barrier_semaphore()
+
+    def greet(to_tm):
+        for to_space in range(n_space):
+            to = (to_tm, to_space)
+            pl.semaphore_signal(barrier, inc=1, device_id=to, device_id_type=MESH)
+
+    @pl.when(tm < last)
+    def _():
+        greet(0)
+
+    for to_tm in range(1, n_tm):
+        greet(to_tm)
+
     fetches = [
-        pltpu.make_async_copy(
-            trans_ref.at[:, pl.ds(first_ray, SUBLANES), :], trans_rows, local_sem.at[0]
-        ),
+        pltpu.make_async_copy(trans_ref, trans_rows, local_sem.at[0]),
         pltpu.make_async_copy(kernel_ref, near_rows, local_sem.at[1]),
         pltpu.make_async_copy(source_ref, sources, local_sem.at[2]),
         pltpu.make_async_copy(near_ref, nears, local_sem.at[3]),
@@ -141,30 +184,70 @@
         pltpu.make_async_copy(signal_ref.at[nth], staged.at[:, nth], stage_sem.at[nth])
         for nth in range(box_dev)
     ]
-    barrier = pltpu.get_barrier_semaphore()
-    for peer in range(peers):
-        to = (peer % n_tm, peer // n_tm)
-        pl.semaphore_signal(barrier, inc=1, device_id=to, device_id_type=MESH)
-    for fetch in stagings:
+    for fetch in stagings + fetches:
         fetch.start()
-    for fetch in fetches:
-        fetch.start()
-    pltpu.make_async_copy(
-        signal_ref.at[:, mine], landed.at[tm + 1, own_boxes], in_recv.at[tm]
-    ).start()
     for staging in stagings:
         staging.wait()
-    pl.semaphore_wait(barrier, peers)
-    for position in reversed(range(peers - 1)):
-        peer = skipping(position, mine)
+
+    def place_of(place):
+        return landed.at[place, own_boxes]
+
+    def send_in(to_tm, to_space, group, place):
         pltpu.make_async_remote_copy(
-            src_ref=staged.at[peer],
-            dst_ref=landed.at[tm + 1, own_boxes],
+            src_ref=staged.at[to_space * n_tm + group],
+            dst_ref=place_of(place),
             send_sem=in_send,
-            recv_sem=in_recv.at[tm],
-            device_id=(peer % n_tm, peer // n_tm),
+            recv_sem=in_recv.at[place],
+            device_id=(to_tm, to_space),
             device_id_type=MESH,
         ).start()
+
+    def keep_in(group, place):
+        source = staged.at[space * n_tm + group]
+        pltpu.make_async_copy(source, place_of(place), in_recv.at[place]).start()
+
+    @pl.when(on_first)
+    def _():
+        pl.semaphore_wait(barrier, last * n_space)
+        for position in reversed(range(last * n_space - 1)):
+            peer = skipping(position, space * last)
+            to_tm, to_space = peer % last, peer // last
+            send_in(to_tm, to_space, to_tm, 1)
+        for position in reversed(range(n_space - 1)):
+            send_in(0, skipping(position, space), last, n_tm)
+        keep_in(0, 1)
+        keep_in(last, n_tm)
+        pl.semaphore_wait(ready, n_space)
+        for to_space in reversed(range(n_space)):
+            send_in(last, to_space, last, 1)
+
+    @pl.when(on_middle)
+    def _():
+        pl.semaphore_wait(barrier, peers)
+        for position in reversed(range(peers - 1)):
+            peer = skipping(position, space * n_tm + tm)
+            to_tm, to_space = peer % n_tm, peer // n_tm
+            send_in(to_tm, to_space, to_tm, tm + 1)
+        keep_in(tm, tm + 1)
+
+        @pl.when(tm == last - 1)
+        def _():
+            for to_space in reversed(range(n_space)):
+                send_in(last, to_space, 0, 0)
+
+    @pl.when(on_last)
+    def _():
+        pl.semaphore_wait(barrier, peers)
+        for to_space in range(n_space):
+            pl.semaphore_signal(ready, inc=1, device_id=(0, to_space), device_id_type=MESH)
+        for position in reversed(range(last * n_space - 1)):
+            peer = skipping(position, space * last + last - 1)
+            to_tm, to_space = peer % last + 1, peer // last
+            send_in(to_tm, to_space, to_tm, n_tm)
+        for position in reversed(range(n_space - 1)):
+            send_in(last, skipping(position, space), 0, n_tm + 1)
+        keep_in(last, n_tm)
+        keep_in(0, n_tm + 1)
 
     for fetch in fetches:
         fetch.wait()
@@ -174,92 +257,145 @@
             lags.astype(jnp.bfloat16), forward[0:LANES, :], preferred_element_type=jnp.float32
         )
 
-    far_real = respond(trans_rows[...].reshape(offsets * SUBLANES, LANES))
-    near_real = respond(near_rows[...])
-    for entry in range(offsets + slots):
-        if entry < offsets:
-            both = far_real[entry * SUBLANES : (entry + 1) * SUBLANES, :]
-        else:
-            slot = entry - offsets
-            both = jnp.broadcast_to(near_real[slot : slot + 1, :], (SUBLANES, 2 * LANES))
+    def keep_response(where, both):
         real, imag = both[:, :LANES], both[:, LANES:]
-        responses[entry, 0] = real
-        responses[entry, 1] = imag - real
-        responses[entry, 2] = imag + real
-    landed[0] = jnp.zeros(landed.shape[1:], jnp.bfloat16)
-
-    def unpacked(block):
-        flat = landed[block].astype(jnp.float32).reshape(boxes * SUBLANES, LANES)
+        where[0] = real
+        where[1] = imag - real
+        where[2] = imag + real
+
+    for turn in range(n_tm):
+        first_ray = pl.multiple_of(group_of(item_at(turn)) * SUBLANES, SUBLANES)
+        far = respond(
+            trans_rows[:, pl.ds(first_ray, SUBLANES), :].reshape(offsets * SUBLANES, LANES)
+        )
+        for entry in range(offsets):
+            these = slice(entry * SUBLANES, (entry + 1) * SUBLANES)
+            keep_response(responses.at[turn, entry], far[these])
+    near = respond(near_rows[...])
+    for slot in range(slots):
+        both = jnp.broadcast_to(near[slot : slot + 1, :], (SUBLANES, 2 * LANES))
+        keep_response(near_responses.at[slot], both)
+
+    def arrive(place):
+        arrived = landed.at[place]
+        pltpu.make_async_copy(arrived, arrived, in_recv.at[place]).wait()
+
+    def unpacked(place):
+        flat = landed[place].astype(jnp.float32).reshape(boxes * SUBLANES, LANES)
         return flat.astype(jnp.bfloat16)
 
-    for block in reversed(range(n_tm)):
-        for arriving in range(block, block - 2, -1):
-            if arriving >= 0 and (arriving < block or block == n_tm - 1):
-                arrived = landed.at[arriving + 1]
-                pltpu.make_async_copy(arrived, arrived, in_recv.at[arriving]).wait()
-        pair = jnp.concatenate([unpacked(block), unpacked(block + 1)], axis=1)
+    def transform(turn):
+        earlier, current = places(item_at(turn))
+        pair = jnp.concatenate([unpacked(earlier), unpacked(current)], axis=1)
         both = jnp.dot(pair, forward[...], preferred_element_type=jnp.float32)
-        spectra[:, 2 * block] = both[:, :LANES].reshape(boxes, SUBLANES, LANES)
-        spectra[:, 2 * block + 1] = both[:, LANES:].reshape(boxes, SUBLANES, LANES)
-
-    def finish(to_space):
-        wanted = [(nth, block) for nth in range(box_dev) for block in range(n_tm)]
-        sums = {}
+        spectra[:, 2 * turn] = both[:, :LANES].reshape(boxes, SUBLANES, LANES)
+        spectra[:, 2 * turn + 1] = both[:, LANES:].reshape(boxes, SUBLANES, LANES)
+
+    def finish(turn, first):
+        targets = [first * box_dev + nth for nth in range(SHARE * box_dev)]
+        sums = [None] * len(targets)
         for entry in range(offsets + slots):
-            factors = [responses[entry, part] for part in range(3)]
-            for nth in range(box_dev):
-                box = to_space * box_dev + nth
+            if entry < offsets:
+                factors = [responses[turn, entry, part] for part in range(3)]
+            else:
+                factors = [near_responses[entry - offsets, part] for part in range(3)]
+            for place, box in enumerate(targets):
                 origin = sources[box, entry] if entry < offsets else nears[entry - offsets, box]
-                for block in range(n_tm):
-                    a, b = (spectra[origin, 2 * block + part] for part in range(2))
-                    terms = [factors[0] * (a + b), factors[1] * a, factors[2] * b]
-                    if entry:
-                        terms = [x + y for x, y in zip(sums[nth, block], terms)]
-                    sums[nth, block] = terms
-        real = jnp.concatenate([sums[w][0] - sums[w][2] for w in wanted], axis=0)
-        imag = jnp.concatenate([sums[w][0] + sums[w][1] for w in wanted], axis=0)
+                a, b = (spectra[origin, 2 * turn + part] for part in range(2))
+                terms = [factors[0] * (a + b), factors[1] * a, factors[2] * b]
+                if entry:
+                    terms = [x + y for x, y in zip(sums[place], terms)]
+                sums[place] = terms
+        real = jnp.concatenate([x - z for x, y, z in sums], axis=0)
+        imag = jnp.concatenate([x + y for x, y, z in sums], axis=0)
         spectrum = jnp.concatenate([real, imag], axis=1).astype(jnp.bfloat16)
         field = jnp.dot(spectrum, inverse[...], preferred_element_type=jnp.float32)
-        for place, (nth, block) in enumerate(wanted):
-            leaving[block, to_space * box_dev + nth] = field[
-                place * SUBLANES : (place + 1) * SUBLANES
-            ].astype(jnp.bfloat16)
-
-    def dispatch(to_space):
-        to_boxes = pl.ds(to_space * box_dev, box_dev)
-
-        def remote(to_tm):
+        for nth, box in enumerate(targets):
+            leaving[turn, box] = field[nth * SUBLANES : (nth + 1) * SUBLANES].astype(jnp.bfloat16)
+
+    def deliver(turn, first):
+        item = item_at(turn)
+        to_tm = jnp.where(swapped(item), tm, item + jnp.where(on_last, 1, 0))
+        target = out_ref.at[:, space * n_tm + group_of(item)]
+        own_line = to_tm == tm
+        own_here = jnp.logical_and(own_line, space // SHARE == first // SHARE)
+
+        def source(to_space):
+            return leaving.at[turn, pl.ds(to_space * box_dev, box_dev)]
+
+        def send_out(to_space):
             pltpu.make_async_remote_copy(
-                src_ref=leaving.at[to_tm, to_boxes],
-                dst_ref=out_ref.at[:, mine],
+                src_ref=source(to_space),
+                dst_ref=target,
                 send_sem=out_send,
                 recv_sem=out_recv,
                 device_id=(to_tm, to_space),
                 device_id_type=MESH,
             ).start()
 
-        for position in range(n_tm - 1):
-            remote(skipping(position, tm))
-
-        @pl.when(space != to_space)
+        @pl.when(jnp.logical_not(own_here))
         def _():
-            remote(tm)
-
-        @pl.when(space == to_space)
+            for nth in range(SHARE):
+                send_out(first + nth)
+
+        @pl.when(own_here)
         def _():
-            pltpu.make_async_copy(leaving.at[tm, to_boxes], out_ref.at[:, mine], out_recv).start()
-
-    def serve(to_space, carry):
-        finish(to_space)
-        dispatch(to_space)
-        return carry
-
-    lax.fori_loop(0, n_space, serve, 0)
-
-    sent = staged.at[pl.ds(0, peers - 1)]
-    pltpu.make_async_copy(sent, sent, in_send).wait()
+            for position in range(SHARE - 1):
+                send_out(first + skipping(position, space - first))
+            pltpu.make_async_copy(source(space), target, out_recv).start()
+
+    @pl.when(tm < last)
+    def _():
+        landed[0] = jnp.zeros(landed.shape[1:], jnp.bfloat16)
+
+    for turn in range(n_tm):
+        for line in range(n_tm):
+            if awaited(line, turn):
+
+                @pl.when(tm == line)
+                def _():
+                    for place in awaited(line, turn):
+                        arrive(place)
+
+        transform(turn)
+
+        def serve(part, carry, turn=turn):
+            finish(turn, part * SHARE)
+            deliver(turn, part * SHARE)
+            return carry
+
+        lax.fori_loop(0, n_space // SHARE, serve, 0)
+
+    def settle(pieces, sem):
+        sent = staged.at[pl.ds(0, pieces)]
+        pltpu.make_async_copy(sent, sent, sem).wait()
+
+    @pl.when(on_first)
+    def _():
+        settle(last * n_space - 1 + n_space - 1, in_send)
+        settle(n_space, in_send)
+
+    @pl.when(on_middle)
+    def _():
+        settle(peers - 1, in_send)
+
+        @pl.when(tm == last - 1)
+        def _():
+            settle(n_space, in_send)
+
+    @pl.when(on_last)
+    def _():
+        settle(last * n_space - 1 + n_space - 1, in_send)
+
     pltpu.make_async_copy(out_ref, out_ref, out_recv).wait()
-    pltpu.make_async_copy(sent, sent, out_send).wait()
+
+    @pl.when(on_middle)
+    def _():
+        settle(peers - 1, out_send)
+
+    @pl.when(on_edge)
+    def _():
+        settle(peers - 2, out_send)
 
 
 def fused_body(signal, source_boxes, near_boxes, trans_kernel, near_kernel):
@@ -282,10 +418,11 @@
         out_specs=pl.BlockSpec(memory_space=pl.ANY),
         scratch_shapes=[
             pltpu.VMEM((peers, box_dev, SUBLANES, LANES), jnp.bfloat16),
-            pltpu.VMEM((n_tm + 1, boxes, SUBLANES, LANES), jnp.bfloat16),
+            pltpu.VMEM((n_tm + 2, boxes, SUBLANES, LANES), jnp.bfloat16),
             pltpu.VMEM((boxes, 2 * n_tm, SUBLANES, LANES), jnp.float32),
-            pltpu.VMEM((offsets + slots, 3, SUBLANES, LANES), jnp.float32),
-            pltpu.VMEM((offsets, SUBLANES, LANES), jnp.float32),
+            pltpu.VMEM((n_tm, offsets, 3, SUBLANES, LANES), jnp.float32),
+            pltpu.VMEM((slots, 3, SUBLANES, LANES), jnp.float32),
+            pltpu.VMEM(trans_kernel.shape, jnp.float32),
             pltpu.VMEM((slots, LANES), jnp.float32),
             pltpu.VMEM(forward.shape, jnp.bfloat16),
             pltpu.VMEM(inverse.shape, jnp.bfloat16),
@@ -293,11 +430,12 @@
             pltpu.SMEM(source_boxes.shape, jnp.int32),
             pltpu.SMEM(near_boxes.shape[::-1], jnp.int32),
             pltpu.SemaphoreType.DMA,
-            pltpu.SemaphoreType.DMA((n_tm,)),
+            pltpu.SemaphoreType.DMA((n_tm + 2,)),
             pltpu.SemaphoreType.DMA,
             pltpu.SemaphoreType.DMA,
             pltpu.SemaphoreType.DMA((6,)),
             pltpu.SemaphoreType.DMA((box_dev,)),
+            pltpu.SemaphoreType.REGULAR,
         ],
         compiler_params=pltpu.CompilerParams(
             collective_id=0, has_side_effects=True, vmem_limit_bytes=60*1024*1024
@@ -310,7 +448,7 @@
     n_tm, n_space = lax.axis_size("tm"), lax.axis_size("space")
     box_dev, rays, samples = signal.shape
     rows = n_tm * n_space * box_dev
-    fits = rays == n_tm * n_space * SUBLANES and samples == LANES and rows <= 2 * LANES
+    fits = n_tm == 4 and n_space % SHARE == 0 and rays == n_tm * n_space * SUBLANES and samples == LANES and rows <= 2 * LANES
     chosen = fused_body if fits else body
     return chosen(signal, source_boxes, near_boxes, trans_kernel, near_kernel)
 

time: 17.6 us -> 16.9 us (0.960)
  the two profiles are of different devices: /device:TPU:0 before, /device:TPU:7 now
where the time goes in v4:
time: 16.9 us; the launch traced here: 16.7 us
  Pallas kernels  16.1 us (95%)
  local copies, waits for them, and re-layouts  0.66 us (4%)
    pallas_call x1, Pallas kernels, fused_body(): pl.pallas_call(functools.partial(fused_kernel, n_tm, n_space), out_shape=...  16.1 us
    unnamed x1, local copies, waits for them, and re-layouts  0.66 us

profile of v4, /device:TPU:7, one launch (start us, length us, event | category | flops | bytes accessed | tf_op | source)
XLA Modules:
  0.0 16.7 jit_solution(14871890670050139013)
XLA Ops:
  0.0 16.1 %shard_map.73 = bf16[2,32,8,128]{3,2,1,0:T(8,128)(2,1)S(1)} custom-call(bf16[2,32,8,128]{3,2,1,0:T(8,128)(2,1)} %bitcast.4, s32[16,12]{1,0:T(8,128)} %source_ref.1, s32[8,16]{1,0:T(8,128)} %bitcast.5, f32[12,32,128]{2,1,0:T(8,128)} %trans_ref.1, f32[8,128]{1,0:T(8,128)} %kernel_ref.1, bf16[256,256]{1,0:T(8,128)(2,1)} %constant.4.clone.forward_ref, ...), custom_call_target="tpu_custom_call" | custom-call | tf_op jit(solution)/shard_map/pallas_call | solution.py:414
  16.1 0.7 %copy.9 = bf16[2,256,128]{2,1,0:T(8,128)(2,1)} copy(bf16[2,256,128]{2,1,0:T(8,128)(2,1)S(1)} %bitcast.3) | data formatting | bytes 262144

commit v5 on v4

--- a/solution.py
+++ b/solution.py
@@ -13,7 +13,7 @@
 LANES = 128
 SUBLANES = 8
 SHARE = 4
-ORDERS = ((0,3,1,2),(0,1,2,3),(0,1,2,3),(1,0,2,3))
+ORDERS = ((0,3,1,2),(0,1,2,3),(0,1,2,3),(1,2,0,3))
 def from_behind(shard, axis, by):
     size = lax.axis_size(axis)
     pairs = [(i, i + by) for i in range(size) if 0 <= i + by < size]
@@ -359,12 +359,9 @@
 
         transform(turn)
 
-        def serve(part, carry, turn=turn):
-            finish(turn, part * SHARE)
-            deliver(turn, part * SHARE)
-            return carry
-
-        lax.fori_loop(0, n_space // SHARE, serve, 0)
+        for first in range(0, n_space, SHARE):
+            finish(turn, first)
+            deliver(turn, first)
 
     def settle(pieces, sem):
         sent = staged.at[pl.ds(0, pieces)]

time: 16.9 us -> 16.4 us (0.970)
  the two profiles are of different devices: /device:TPU:7 before, /device:TPU:3 now
where the time goes in v5:
time: 16.4 us; the launch traced here: 16.3 us
  Pallas kernels  15.6 us (95%)
  local copies, waits for them, and re-layouts  0.66 us (4%)
    pallas_call x1, Pallas kernels, fused_body(): pl.pallas_call(functools.partial(fused_kernel, n_tm, n_space), out_shape=...  15.6 us
    unnamed x1, local copies, waits for them, and re-layouts  0.66 us

profile of v5, /device:TPU:3, one launch (start us, length us, event | category | flops | bytes accessed | tf_op | source)
XLA Modules:
  0.0 16.3 jit_solution(13000171441355673194)
XLA Ops:
  0.0 15.6 %shard_map.73 = bf16[2,32,8,128]{3,2,1,0:T(8,128)(2,1)S(1)} custom-call(bf16[2,32,8,128]{3,2,1,0:T(8,128)(2,1)} %bitcast.4, s32[16,12]{1,0:T(8,128)} %source_ref.1, s32[8,16]{1,0:T(8,128)} %bitcast.5, f32[12,32,128]{2,1,0:T(8,128)} %trans_ref.1, f32[8,128]{1,0:T(8,128)} %kernel_ref.1, bf16[256,256]{1,0:T(8,128)(2,1)} %constant.4.clone.forward_ref, ...), custom_call_target="tpu_custom_call" | custom-call | tf_op jit(solution)/shard_map/pallas_call | solution.py:411
  15.6 0.7 %copy.9 = bf16[2,256,128]{2,1,0:T(8,128)(2,1)} copy(bf16[2,256,128]{2,1,0:T(8,128)(2,1)S(1)} %bitcast.3) | data formatting | bytes 262144

commit v6 on v5

--- a/solution.py
+++ b/solution.py
@@ -210,7 +210,8 @@
     def _():
         pl.semaphore_wait(barrier, last * n_space)
         for position in reversed(range(last * n_space - 1)):
-            peer = skipping(position, space * last)
+            far = last * n_space - 2 - position
+            peer = skipping(jnp.where(space < n_space // 2, position, far), space * last)
             to_tm, to_space = peer % last, peer // last
             send_in(to_tm, to_space, to_tm, 1)
         for position in reversed(range(n_space - 1)):
@@ -225,7 +226,8 @@
     def _():
         pl.semaphore_wait(barrier, peers)
         for position in reversed(range(peers - 1)):
-            peer = skipping(position, space * n_tm + tm)
+            place = jnp.where(space < n_space // 2, position, peers - 2 - position)
+            peer = skipping(place, space * n_tm + tm)
             to_tm, to_space = peer % n_tm, peer // n_tm
             send_in(to_tm, to_space, to_tm, tm + 1)
         keep_in(tm, tm + 1)
@@ -241,7 +243,8 @@
         for to_space in range(n_space):
             pl.semaphore_signal(ready, inc=1, device_id=(0, to_space), device_id_type=MESH)
         for position in reversed(range(last * n_space - 1)):
-            peer = skipping(position, space * last + last - 1)
+            far = last * n_space - 2 - position
+            peer = skipping(jnp.where(space < n_space // 2, position, far), space * last + last - 1)
             to_tm, to_space = peer % last + 1, peer // last
             send_in(to_tm, to_space, to_tm, n_tm)
         for position in reversed(range(n_space - 1)):
@@ -291,8 +294,8 @@
         spectra[:, 2 * turn] = both[:, :LANES].reshape(boxes, SUBLANES, LANES)
         spectra[:, 2 * turn + 1] = both[:, LANES:].reshape(boxes, SUBLANES, LANES)
 
-    def finish(turn, first):
-        targets = [first * box_dev + nth for nth in range(SHARE * box_dev)]
+    def finish(turn, first, end):
+        targets = list(range(first * box_dev, end * box_dev))
         sums = [None] * len(targets)
         for entry in range(offsets + slots):
             if entry < offsets:
@@ -313,12 +316,13 @@
         for nth, box in enumerate(targets):
             leaving[turn, box] = field[nth * SUBLANES : (nth + 1) * SUBLANES].astype(jnp.bfloat16)
 
-    def deliver(turn, first):
+    def deliver(turn, first, end):
         item = item_at(turn)
         to_tm = jnp.where(swapped(item), tm, item + jnp.where(on_last, 1, 0))
         target = out_ref.at[:, space * n_tm + group_of(item)]
         own_line = to_tm == tm
-        own_here = jnp.logical_and(own_line, space // SHARE == first // SHARE)
+        here = jnp.logical_and(space >= first, space < end)
+        own_here = jnp.logical_and(own_line, here)
 
         def source(to_space):
             return leaving.at[turn, pl.ds(to_space * box_dev, box_dev)]
@@ -335,20 +339,20 @@
 
         @pl.when(jnp.logical_not(own_here))
         def _():
-            for nth in range(SHARE):
-                send_out(first + nth)
+            for to_space in range(first, end):
+                send_out(to_space)
 
         @pl.when(own_here)
         def _():
-            for position in range(SHARE - 1):
-                send_out(first + skipping(position, space - first))
+            for position in range(first, end - 1):
+                send_out(skipping(position, space))
             pltpu.make_async_copy(source(space), target, out_recv).start()
 
     @pl.when(tm < last)
     def _():
         landed[0] = jnp.zeros(landed.shape[1:], jnp.bfloat16)
 
-    for turn in range(n_tm):
+    def take(turn):
         for line in range(n_tm):
             if awaited(line, turn):
 
@@ -359,9 +363,20 @@
 
         transform(turn)
 
-        for first in range(0, n_space, SHARE):
-            finish(turn, first)
-            deliver(turn, first)
+    def serve(turn, *shares):
+        for first, end in shares:
+            finish(turn, first, end)
+            deliver(turn, first, end)
+
+    near, rest = [(0, 4)], [(4, n_space)]
+    for turn in range(2):
+        take(turn)
+        serve(turn, *near, *rest)
+    for turn in range(2, n_tm):
+        take(turn)
+        serve(turn, *near)
+    for turn in range(2, n_tm):
+        serve(turn, *rest)
 
     def settle(pieces, sem):
         sent = staged.at[pl.ds(0, pieces)]

time: 16.4 us -> 16.4 us (level)
  the two profiles are of different devices: /device:TPU:3 before, /device:TPU:19 now
where the time goes in v6:
time: 16.4 us; the launch traced here: 16.3 us
  Pallas kernels  15.6 us (95%)
  local copies, waits for them, and re-layouts  0.66 us (4%)
    pallas_call x1, Pallas kernels, fused_body(): pl.pallas_call(functools.partial(fused_kernel, n_tm, n_space), out_shape=...  15.6 us
    unnamed x1, local copies, waits for them, and re-layouts  0.66 us

profile of v6, /device:TPU:19, one launch (start us, length us, event | category | flops | bytes accessed | tf_op | source)
XLA Modules:
  0.0 16.3 jit_solution(9929194596402663476)
XLA Ops:
  0.0 15.6 %shard_map.73 = bf16[2,32,8,128]{3,2,1,0:T(8,128)(2,1)S(1)} custom-call(bf16[2,32,8,128]{3,2,1,0:T(8,128)(2,1)} %bitcast.4, s32[16,12]{1,0:T(8,128)} %source_ref.1, s32[8,16]{1,0:T(8,128)} %bitcast.5, f32[12,32,128]{2,1,0:T(8,128)} %trans_ref.1, f32[8,128]{1,0:T(8,128)} %kernel_ref.1, bf16[256,256]{1,0:T(8,128)(2,1)} %constant.4.clone.forward_ref, ...), custom_call_target="tpu_custom_call" | custom-call | tf_op jit(solution)/shard_map/pallas_call | solution.py:426
  15.6 0.7 %copy.9 = bf16[2,256,128]{2,1,0:T(8,128)(2,1)} copy(bf16[2,256,128]{2,1,0:T(8,128)(2,1)S(1)} %bitcast.3) | data formatting | bytes 262144

commit v7 on v5

--- a/solution.py
+++ b/solution.py
@@ -12,7 +12,7 @@
 MESH = pl.DeviceIdType.MESH
 LANES = 128
 SUBLANES = 8
-SHARE = 4
+SHARE = 8
 ORDERS = ((0,3,1,2),(0,1,2,3),(0,1,2,3),(1,2,0,3))
 def from_behind(shard, axis, by):
     size = lax.axis_size(axis)
@@ -210,7 +210,8 @@
     def _():
         pl.semaphore_wait(barrier, last * n_space)
         for position in reversed(range(last * n_space - 1)):
-            peer = skipping(position, space * last)
+            far = last * n_space - 2 - position
+            peer = skipping(jnp.where(space < n_space // 2, position, far), space * last)
             to_tm, to_space = peer % last, peer // last
             send_in(to_tm, to_space, to_tm, 1)
         for position in reversed(range(n_space - 1)):
@@ -225,7 +226,8 @@
     def _():
         pl.semaphore_wait(barrier, peers)
         for position in reversed(range(peers - 1)):
-            peer = skipping(position, space * n_tm + tm)
+            place = jnp.where(space < n_space // 2, position, peers - 2 - position)
+            peer = skipping(place, space * n_tm + tm)
             to_tm, to_space = peer % n_tm, peer // n_tm
             send_in(to_tm, to_space, to_tm, tm + 1)
         keep_in(tm, tm + 1)
@@ -241,7 +243,8 @@
         for to_space in range(n_space):
             pl.semaphore_signal(ready, inc=1, device_id=(0, to_space), device_id_type=MESH)
         for position in reversed(range(last * n_space - 1)):
-            peer = skipping(position, space * last + last - 1)
+            far = last * n_space - 2 - position
+            peer = skipping(jnp.where(space < n_space // 2, position, far), space * last + last - 1)
             to_tm, to_space = peer % last + 1, peer // last
             send_in(to_tm, to_space, to_tm, n_tm)
         for position in reversed(range(n_space - 1)):

time: 16.4 us -> 16.5 us (level)
  no operation moved by 1% of the time
where the time goes in v7:
time: 16.5 us; the launch traced here: 16.4 us
  Pallas kernels  15.7 us (95%)
  local copies, waits for them, and re-layouts  0.66 us (4%)
    pallas_call x1, Pallas kernels, fused_body(): pl.pallas_call(functools.partial(fused_kernel, n_tm, n_space), out_shape=...  15.7 us
    unnamed x1, local copies, waits for them, and re-layouts  0.66 us

profile of v7, /device:TPU:3, one launch (start us, length us, event | category | flops | bytes accessed | tf_op | source)
XLA Modules:
  0.0 16.4 jit_solution(4249467415651264894)
XLA Ops:
  0.0 15.7 %shard_map.73 = bf16[2,32,8,128]{3,2,1,0:T(8,128)(2,1)S(1)} custom-call(bf16[2,32,8,128]{3,2,1,0:T(8,128)(2,1)} %bitcast.4, s32[16,12]{1,0:T(8,128)} %source_ref.1, s32[8,16]{1,0:T(8,128)} %bitcast.5, f32[12,32,128]{2,1,0:T(8,128)} %trans_ref.1, f32[8,128]{1,0:T(8,128)} %kernel_ref.1, bf16[256,256]{1,0:T(8,128)(2,1)} %constant.4.clone.forward_ref, ...), custom_call_target="tpu_custom_call" | custom-call | tf_op jit(solution)/shard_map/pallas_call | solution.py:414
  15.7 0.7 %copy.9 = bf16[2,256,128]{2,1,0:T(8,128)(2,1)} copy(bf16[2,256,128]{2,1,0:T(8,128)(2,1)S(1)} %bitcast.3) | data formatting | bytes 262144
